TPU v7x, 512 devices: a whole 4x8x8 slice. The times are simulated.
512 devices in a mesh: pa: 8 (over y), pb: 64 (over z, x, core).
Axes of the slice: x: 4, y: 8, z: 8, core: 2. Of those that a mesh axis runs over, the one named last changes fastest.
Arguments:
- matrix: bfloat16 [12288, 24576], P('pa', 'pb'), may hold values from -6 to 6
- panels: bfloat16 [6, 12288, 128], P(None, ('pa', 'pb')), may hold values from -0.25 to 0.25
- inverses: float32 [6, 128, 128], replicated, as said below
- pivots: int32 [6, 128], replicated, may hold values from 128 to 12287, as said below
Outputs:
- factored: bfloat16 [12288, 24576], P('pa', 'pb')
Inputs may be any that keep to these rules, and one draw needn't show every extreme that they name: `pivots`: row k lists 128 different row numbers, each at least (k + 1) * 128. `inverses`: each block is unit lower triangular.
All inputs are finite; a program needn't handle non-finite values.
Results may differ from a plain program's by a relative error of at most 0.0082.
Values may be sent and summed in bfloat16 or wider, within the bound.
No kernel may reach another device: no remote copies, remote signals or barrier semaphores. Data moves between devices by JAX's collectives and lax.ppermute only.
A program may use at most 64 MiB of HBM per device.

v0:
```python
import jax
import jax.numpy as jnp
from jax import lax
from jax.sharding import PartitionSpec as P

NB = 128
STEPS = 6


def broadcast(x, axis, root):
    mine = lax.axis_index(axis) == root
    return lax.psum(jnp.where(mine, x, jnp.zeros_like(x)), axis)


def per_device(matrix, panels, inverses, pivots):
    local_rows = matrix.shape[0]
    proc_row = lax.axis_index("pa")
    first_row = proc_row * local_rows
    is_owner = proc_row == 0
    global_rows = first_row + jnp.arange(local_rows, dtype=jnp.int32)
    for step in range(STEPS):
        lo = step * NB
        hi = lo + NB
        chosen = pivots[step]
        local_idx = chosen - first_row
        owned = (local_idx >= 0) & (local_idx < local_rows)
        safe_idx = jnp.clip(local_idx, 0, local_rows - 1)
        candidates = jnp.where(
            owned[:, None], jnp.take(matrix, safe_idx, axis=0), jnp.zeros((), jnp.bfloat16)
        )
        top_local = matrix[lo:hi]
        new_top = lax.psum(candidates, "pa").astype(jnp.float32).astype(jnp.bfloat16)
        upper_here = jnp.dot(
            inverses[step],
            new_top.astype(jnp.float32),
            precision=lax.Precision.HIGHEST,
            preferred_element_type=jnp.float32,
        ).astype(jnp.bfloat16)
        upper, old_top = (broadcast(upper_here, "pa", 0), broadcast(top_local, "pa", 0))
        target = jnp.where(owned, local_idx, local_rows)
        matrix = matrix.at[target].set(old_top, mode="drop")
        product = jnp.dot(
            lax.all_gather(panels[step], "pb", axis=0, tiled=True),
            upper,
            preferred_element_type=jnp.float32,
        )
        updated = (matrix.astype(jnp.float32) - product).astype(jnp.bfloat16)
        matrix = jnp.where((global_rows >= hi)[:, None], updated, matrix)
        matrix = matrix.at[lo:hi].set(jnp.where(is_owner, upper, matrix[lo:hi]))
    return matrix


def solution(mesh):
    in_specs = (P("pa", "pb"), P(None, ("pa", "pb"), None), P(), P())
    out_specs = P("pa", "pb")
    return jax.shard_map(
        per_device, mesh=mesh, in_specs=in_specs, out_specs=out_specs, check_vma=False
    )
```

profile of v0, /device:TPU:2, one launch (start us, length us, event | category | flops | bytes accessed | tf_op | source)
XLA Modules:
  0.0 992.1 jit_solution(16481884863507782826)
XLA Ops:
  15.7 57.5 %all-gather = bf16[1,1536,128]{2,1,0:T(8,128)(2,1)} all-gather(bf16[1,24,128]{2,1,0:T(8,128)(2,1)S(1)} %get-tuple-element.106), channel_id=2, replica_groups=mesh['pa'=8,'pb'=64] {'pb'}, dimensions={1}, use_global_device_ids=true | all-gather | bytes 399360 | tf_op jit(solution)/shard_map/all_gather | solution.py:43
  73.2 19.3 %all-reduce.19.cloned.1.call-done = bf16[128,384]{0,1:T(8,128)(2,1)} async-done(((bf16[128,384]{0,1:T(8,128)(2,1)}), bf16[128,384]{0,1:T(8,128)(2,1)}) %all-reduce.19.cloned.1.call-update) | async-done | bytes 98320 | tf_op jit(solution)/shard_map/psum | solution.py:32
  92.5 1.8 fusion.19
  95.0 75.9 %all-reduce.41.cloned.1.call-done = (bf16[128,384]{0,1:T(8,128)(2,1)}, bf16[128,384]{0,1:T(8,128)(2,1)}) async-done(((bf16[128,384]{0,1:T(8,128)(2,1)}, bf16[128,384]{0,1:T(8,128)(2,1)}), (bf16[128,384]{0,1:T(8,128)(2,1)}, bf16[128,384]{0,1:T(8,128)(2,1)})) %all-reduce.41.cloned.1.call-update) | async-done | bytes 196624 | tf_op jit(solution)/shard_map/psum | solution.py:12
  179.2 75.1 %all-reduce.21.cloned.1.call-done = bf16[128,384]{0,1:T(8,128)(2,1)} async-done(((bf16[128,384]{0,1:T(8,128)(2,1)}), bf16[128,384]{0,1:T(8,128)(2,1)}) %all-reduce.21.cloned.1.call-update) | async-done | bytes 98320 | tf_op jit(solution)/shard_map/psum | solution.py:32
  254.4 1.8 fusion.21
  256.2 53.6 %all-gather.1 = bf16[1,1536,128]{2,1,0:T(8,128)(2,1)} all-gather(bf16[1,24,128]{2,1,0:T(8,128)(2,1)S(1)} %copy-done.9), channel_id=3, replica_groups=mesh['pa'=8,'pb'=64] {'pb'}, dimensions={1}, use_global_device_ids=true | all-gather | bytes 399360 | tf_op jit(solution)/shard_map/all_gather | solution.py:43
  310.5 22.2 %all-reduce.39.cloned.1.call-done = (bf16[128,384]{0,1:T(8,128)(2,1)}, bf16[128,384]{0,1:T(8,128)(2,1)}) async-done(((bf16[128,384]{0,1:T(8,128)(2,1)}, bf16[128,384]{0,1:T(8,128)(2,1)}), (bf16[128,384]{0,1:T(8,128)(2,1)}, bf16[128,384]{0,1:T(8,128)(2,1)})) %all-reduce.39.cloned.1.call-update) | async-done | bytes 196624 | tf_op jit(solution)/shard_map/psum | solution.py:12
  341.0 75.2 %all-reduce.23.cloned.1.call-done = bf16[128,384]{0,1:T(8,128)(2,1)} async-done(((bf16[128,384]{0,1:T(8,128)(2,1)}), bf16[128,384]{0,1:T(8,128)(2,1)}) %all-reduce.23.cloned.1.call-update) | async-done | bytes 98320 | tf_op jit(solution)/shard_map/psum | solution.py:32
  416.1 1.8 fusion.23
  418.0 53.8 %all-gather.2 = bf16[1,1536,128]{2,1,0:T(8,128)(2,1)} all-gather(bf16[1,24,128]{2,1,0:T(8,128)(2,1)S(1)} %copy-done.8), channel_id=4, replica_groups=mesh['pa'=8,'pb'=64] {'pb'}, dimensions={1}, use_global_device_ids=true | all-gather | bytes 399360 | tf_op jit(solution)/shard_map/all_gather | solution.py:43
  472.4 22.0 %all-reduce.37.cloned.1.call-done = (bf16[128,384]{0,1:T(8,128)(2,1)}, bf16[128,384]{0,1:T(8,128)(2,1)}) async-done(((bf16[128,384]{0,1:T(8,128)(2,1)}, bf16[128,384]{0,1:T(8,128)(2,1)}), (bf16[128,384]{0,1:T(8,128)(2,1)}, bf16[128,384]{0,1:T(8,128)(2,1)})) %all-reduce.37.cloned.1.call-update) | async-done | bytes 196624 | tf_op jit(solution)/shard_map/psum | solution.py:12
  502.7 75.2 %all-reduce.25.cloned.1.call-done = bf16[128,384]{0,1:T(8,128)(2,1)} async-done(((bf16[128,384]{0,1:T(8,128)(2,1)}), bf16[128,384]{0,1:T(8,128)(2,1)}) %all-reduce.25.cloned.1.call-update) | async-done | bytes 98320 | tf_op jit(solution)/shard_map/psum | solution.py:32
  577.9 1.8 fusion.25
  579.7 53.6 %all-gather.3 = bf16[1,1536,128]{2,1,0:T(8,128)(2,1)} all-gather(bf16[1,24,128]{2,1,0:T(8,128)(2,1)S(1)} %copy-done.7), channel_id=5, replica_groups=mesh['pa'=8,'pb'=64] {'pb'}, dimensions={1}, use_global_device_ids=true | all-gather | bytes 399360 | tf_op jit(solution)/shard_map/all_gather | solution.py:43
  633.9 22.3 %all-reduce.35.cloned.1.call-done = (bf16[128,384]{0,1:T(8,128)(2,1)}, bf16[128,384]{0,1:T(8,128)(2,1)}) async-done(((bf16[128,384]{0,1:T(8,128)(2,1)}, bf16[128,384]{0,1:T(8,128)(2,1)}), (bf16[128,384]{0,1:T(8,128)(2,1)}, bf16[128,384]{0,1:T(8,128)(2,1)})) %all-reduce.35.cloned.1.call-update) | async-done | bytes 196624 | tf_op jit(solution)/shard_map/psum | solution.py:12
  664.6 75.1 %all-reduce.27.cloned.1.call-done = bf16[128,384]{0,1:T(8,128)(2,1)} async-done(((bf16[128,384]{0,1:T(8,128)(2,1)}), bf16[128,384]{0,1:T(8,128)(2,1)}) %all-reduce.27.cloned.1.call-update) | async-done | bytes 98320 | tf_op jit(solution)/shard_map/psum | solution.py:32
  739.7 1.8 fusion.27
  741.6 53.8 %all-gather.4 = bf16[1,1536,128]{2,1,0:T(8,128)(2,1)} all-gather(bf16[1,24,128]{2,1,0:T(8,128)(2,1)S(1)} %get-tuple-element.107), channel_id=6, replica_groups=mesh['pa'=8,'pb'=64] {'pb'}, dimensions={1}, use_global_device_ids=true | all-gather | bytes 399360 | tf_op jit(solution)/shard_map/all_gather | solution.py:43
  795.4 22.5 %all-reduce.33.cloned.1.call-done = (bf16[128,384]{0,1:T(8,128)(2,1)}, bf16[128,384]{0,1:T(8,128)(2,1)}) async-done(((bf16[128,384]{0,1:T(8,128)(2,1)}, bf16[128,384]{0,1:T(8,128)(2,1)}), (bf16[128,384]{0,1:T(8,128)(2,1)}, bf16[128,384]{0,1:T(8,128)(2,1)})) %all-reduce.33.cloned.1.call-update) | async-done | bytes 196624 | tf_op jit(solution)/shard_map/psum | solution.py:12
  826.2 75.2 %all-reduce.29.cloned.1.call-done = bf16[128,384]{0,1:T(8,128)(2,1)} async-done(((bf16[128,384]{0,1:T(8,128)(2,1)}), bf16[128,384]{0,1:T(8,128)(2,1)}) %all-reduce.29.cloned.1.call-update) | async-done | bytes 98320 | tf_op jit(solution)/shard_map/psum | solution.py:32
  901.4 1.8 fusion.29
  903.2 49.0 %all-gather.5 = bf16[1,1536,128]{2,1,0:T(8,128)(2,1)S(1)} all-gather(bf16[1,24,128]{2,1,0:T(8,128)(2,1)S(1)} %get-tuple-element.102), channel_id=7, replica_groups=mesh['pa'=8,'pb'=64] {'pb'}, dimensions={1}, use_global_device_ids=true | all-gather | bytes 399360 | tf_op jit(solution)/shard_map/all_gather | solution.py:43
  952.2 27.4 %all-reduce.31.cloned.1.call-done = (bf16[128,384]{0,1:T(8,128)(2,1)}, bf16[128,384]{0,1:T(8,128)(2,1)}) async-done(((bf16[128,384]{0,1:T(8,128)(2,1)}, bf16[128,384]{0,1:T(8,128)(2,1)}), (bf16[128,384]{0,1:T(8,128)(2,1)}, bf16[128,384]{0,1:T(8,128)(2,1)})) %all-reduce.31.cloned.1.call-update) | async-done | bytes 196624 | tf_op jit(solution)/shard_map/psum | solution.py:12
  (165 shorter events, 58.4 us)
Async XLA Ops:
  6.5 86.0 %all-reduce.19.cloned.1.call-start = ((), (), s32[]{:S(2)}) async-start(), calls=%async_computation | async-start | bytes 196608 | tf_op jit(solution)/shard_map/psum | solution.py:32
  10.7 160.2 %all-reduce.41.cloned.1.call-start = ((), (), s32[]{:S(2)}) async-start(), calls=%async_computation.11 | async-start | bytes 393216 | tf_op jit(solution)/shard_map/psum | solution.py:12
  94.3 160.1 %all-reduce.21.cloned.1.call-start = ((), (), s32[]{:S(2)}) async-start(), calls=%async_computation.1 | async-start | bytes 196608 | tf_op jit(solution)/shard_map/psum | solution.py:32
  176.7 79.5 %copy-start.9 = (bf16[1,24,128]{2,1,0:T(8,128)(2,1)S(1)}, bf16[1,24,128]{2,1,0:T(8,128)(2,1)}, u32[]{:S(2)}) copy-start(bf16[1,24,128]{2,1,0:T(8,128)(2,1)} %get-tuple-element.105) | copy-start | bytes 18436
  176.7 133.2 %copy-start.30 = (s32[128]{0:T(128)S(1)}, s32[128]{0:T(128)}, u32[]{:S(2)}) copy-start(s32[128]{0:T(128)} %get-tuple-element.119) | copy-start | bytes 1540
  176.7 156.9 %copy-start.26 = (s32[128]{0:T(128)S(1)}, s32[128]{0:T(128)}, u32[]{:S(2)}) copy-start(s32[128]{0:T(128)} %get-tuple-element.125) | copy-start | bytes 1540
  178.5 154.1 %all-reduce.39.cloned.1.call-start = ((), (), s32[]{:S(2)}) async-start(), calls=%async_computation.10 | async-start | bytes 393216 | tf_op jit(solution)/shard_map/psum | solution.py:12
  256.2 159.9 %all-reduce.23.cloned.1.call-start = ((), (), s32[]{:S(2)}) async-start(), calls=%async_computation.2 | async-start | bytes 196608 | tf_op jit(solution)/shard_map/psum | solution.py:32
  338.4 79.5 %copy-start.8 = (bf16[1,24,128]{2,1,0:T(8,128)(2,1)S(1)}, bf16[1,24,128]{2,1,0:T(8,128)(2,1)}, u32[]{:S(2)}) copy-start(bf16[1,24,128]{2,1,0:T(8,128)(2,1)} %get-tuple-element.104) | copy-start | bytes 18436
  338.4 133.3 %copy-start.29 = (s32[128]{0:T(128)S(1)}, s32[128]{0:T(128)}, u32[]{:S(2)}) copy-start(s32[128]{0:T(128)} %get-tuple-element.117) | copy-start | bytes 1540
  338.5 156.9 %copy-start.24 = (s32[128]{0:T(128)S(1)}, s32[128]{0:T(128)}, u32[]{:S(2)}) copy-start(s32[128]{0:T(128)} %get-tuple-element.126) | copy-start | bytes 1540
  340.3 154.1 %all-reduce.37.cloned.1.call-start = ((), (), s32[]{:S(2)}) async-start(), calls=%async_computation.9 | async-start | bytes 393216 | tf_op jit(solution)/shard_map/psum | solution.py:12
  417.9 159.9 %all-reduce.25.cloned.1.call-start = ((), (), s32[]{:S(2)}) async-start(), calls=%async_computation.3 | async-start | bytes 196608 | tf_op jit(solution)/shard_map/psum | solution.py:32
  500.2 79.5 %copy-start.7 = (bf16[1,24,128]{2,1,0:T(8,128)(2,1)S(1)}, bf16[1,24,128]{2,1,0:T(8,128)(2,1)}, u32[]{:S(2)}) copy-start(bf16[1,24,128]{2,1,0:T(8,128)(2,1)} %get-tuple-element.103) | copy-start | bytes 18436
  500.2 133.2 %copy-start.28 = (s32[128]{0:T(128)S(1)}, s32[128]{0:T(128)}, u32[]{:S(2)}) copy-start(s32[128]{0:T(128)} %get-tuple-element.115) | copy-start | bytes 1540
  500.2 157.1 %copy-start.22 = (s32[128]{0:T(128)S(1)}, s32[128]{0:T(128)}, u32[]{:S(2)}) copy-start(s32[128]{0:T(128)} %get-tuple-element.127) | copy-start | bytes 1540
  502.0 154.2 %all-reduce.35.cloned.1.call-start = ((), (), s32[]{:S(2)}) async-start(), calls=%async_computation.8 | async-start | bytes 393216 | tf_op jit(solution)/shard_map/psum | solution.py:12
  579.7 160.1 %all-reduce.27.cloned.1.call-start = ((), (), s32[]{:S(2)}) async-start(), calls=%async_computation.4 | async-start | bytes 196608 | tf_op jit(solution)/shard_map/psum | solution.py:32
  662.1 133.4 %copy-start.27 = (s32[128]{0:T(128)S(1)}, s32[128]{0:T(128)}, u32[]{:S(2)}) copy-start(s32[128]{0:T(128)} %get-tuple-element.91) | copy-start | bytes 1540
  662.1 156.9 %copy-start.20 = (s32[128]{0:T(128)S(1)}, s32[128]{0:T(128)}, u32[]{:S(2)}) copy-start(s32[128]{0:T(128)} %get-tuple-element.128) | copy-start | bytes 1540
  663.9 154.1 %all-reduce.33.cloned.1.call-start = ((), (), s32[]{:S(2)}) async-start(), calls=%async_computation.7 | async-start | bytes 393216 | tf_op jit(solution)/shard_map/psum | solution.py:12
  741.5 159.8 %all-reduce.29.cloned.1.call-start = ((), (), s32[]{:S(2)}) async-start(), calls=%async_computation.5 | async-start | bytes 196608 | tf_op jit(solution)/shard_map/psum | solution.py:32
  823.8 156.8 %copy-start.18 = (s32[128]{0:T(128)S(1)}, s32[128]{0:T(128)}, u32[]{:S(2)}) copy-start(s32[128]{0:T(128)} %get-tuple-element.124) | copy-start | bytes 1540
  825.5 154.1 %all-reduce.31.cloned.1.call-start = ((), (), s32[]{:S(2)}) async-start(), calls=%async_computation.6 | async-start | bytes 393216 | tf_op jit(solution)/shard_map/psum | solution.py:12
  (19 other events, 34.8 us)
Sparse Core Ops, SparseCore 0:
  10.8 81.6 all-reduce.18
  95.0 75.9 all-reduce.40
  178.7 75.6 all-reduce.20
  256.7 75.9 all-reduce.38
  340.4 75.6 all-reduce.22
  418.4 75.9 all-reduce.36
  502.1 75.6 all-reduce.24
  580.3 75.9 all-reduce.34
  664.0 75.6 all-reduce.26
  742.0 75.9 all-reduce.32
  825.6 75.6 all-reduce.28
  903.7 75.9 all-reduce.30
where the time goes:
time: 993 us; the launch traced here: 992 us
  waiting for transfers between devices  588 us (59%)
  blocking collectives  321 us (32%)
  local copies, waits for them, and re-layouts  34.2 us (3%)
  matrix products  18.7 us (2%)
  other arithmetic  15.4 us (2%)
  between operations  14.3 us (1%)
    psum x6, waiting for transfers between devices, per_device(): lax.psum(candidates, 'pa').astype(jnp.float32).astype(jnp.bfloat16)  395 us
    all_gather x6, blocking collectives, per_device(): lax.all_gather(panels[step], 'pb', axis=0, tiled=True)  321 us
    psum x6, waiting for transfers between devices, broadcast(): return lax.psum(jnp.where(mine, x, jnp.zeros_like(x)), axis)  192 us
  transfers between devices with their start and end apart: 12, of which 12 were waited for; matrix products, arithmetic and copies ran while one was open for 1% of the time, Pallas kernels for 0%

commit v1 on v0

--- a/solution.py
+++ b/solution.py
@@ -29,7 +29,11 @@
             owned[:, None], jnp.take(matrix, safe_idx, axis=0), jnp.zeros((), jnp.bfloat16)
         )
         top_local = matrix[lo:hi]
-        new_top = lax.psum(candidates, "pa").astype(jnp.float32).astype(jnp.bfloat16)
+        new_top = (
+            jnp.sum(lax.all_gather(candidates, "pa"), axis=0)
+            .astype(jnp.float32)
+            .astype(jnp.bfloat16)
+        )
         upper_here = jnp.dot(
             inverses[step],
             new_top.astype(jnp.float32),

time: 993 us -> 700 us (0.70)
  waiting for transfers between devices: 588 us -> 136 us
  blocking collectives: 321 us -> 471 us
    psum x6 -> x0, waiting for transfers between devices: 395 us -> none  [per_device(): lax.psum(candidates, 'pa').astype(jnp.float32).astype(jnp.bfloat16)]
    all_gather x0 -> x6, blocking collectives: none -> 150 us  [per_device(): lax.all_gather(candidates, 'pa')]
    psum x6, waiting for transfers between devices: 192 us -> 136 us  [broadcast(): return lax.psum(jnp.where(mine, x, jnp.zeros_like(x)), axis)]
  transfers between devices with their start and end apart: 12 -> 6, of which waited for: 12 -> 6; matrix products, arithmetic and copies ran while one was open for 1% -> 1% of each run, Pallas kernels for 0% -> 0%
where the time goes in v1:
time: 700 us; the launch traced here: 691 us
  blocking collectives  471 us (67%)
  waiting for transfers between devices  136 us (19%)
  local copies, waits for them, and re-layouts  35.6 us (5%)
  matrix products  18.4 us (3%)
  other arithmetic  15.2 us (2%)
  between operations  14.7 us (2%)
    all_gather x6, blocking collectives, per_device(): lax.all_gather(panels[step], 'pb', axis=0, tiled=True)  321 us
    all_gather x6, blocking collectives, per_device(): lax.all_gather(candidates, 'pa')  150 us
    psum x6, waiting for transfers between devices, broadcast(): return lax.psum(jnp.where(mine, x, jnp.zeros_like(x)), axis)  136 us
    scatter x12, local copies, waits for them, and re-layouts, per_device(): matrix = matrix.at[target].set(old_top, mode='drop')  14.7 us
  transfers between devices with their start and end apart: 6, of which 6 were waited for; matrix products, arithmetic and copies ran while one was open for 1% of the time, Pallas kernels for 0%

profile of v1, /device:TPU:2, one launch (start us, length us, event | category | flops | bytes accessed | tf_op | source)
XLA Modules:
  0.0 690.9 jit_solution(10344121167047682234)
XLA Ops:
  10.2 27.7 %all-gather = bf16[1024,384]{0,1:T(8,128)(2,1)S(1)} all-gather(bf16[128,384]{0,1:T(8,128)(2,1)S(1)} %select_select_fusion.5), channel_id=2, replica_groups=mesh['pa'=8,'pb'=64] {'pa'}, dimensions={0}, use_global_device_ids=true | all-gather | bytes 884736 | tf_op jit(solution)/shard_map/all_gather | solution.py:33
  44.7 57.5 %all-gather.1 = bf16[1,1536,128]{2,1,0:T(8,128)(2,1)} all-gather(bf16[1,24,128]{2,1,0:T(8,128)(2,1)S(1)} %get-tuple-element.106), channel_id=3, replica_groups=mesh['pa'=8,'pb'=64] {'pb'}, dimensions={1}, use_global_device_ids=true | all-gather | bytes 399360 | tf_op jit(solution)/shard_map/all_gather | solution.py:47
  103.4 16.8 %all-reduce.23.cloned.1.call-done = (bf16[128,384]{0,1:T(8,128)(2,1)}, bf16[128,384]{0,1:T(8,128)(2,1)}) async-done(((bf16[128,384]{0,1:T(8,128)(2,1)}, bf16[128,384]{0,1:T(8,128)(2,1)}), (bf16[128,384]{0,1:T(8,128)(2,1)}, bf16[128,384]{0,1:T(8,128)(2,1)})) %all-reduce.23.cloned.1.call-update) | async-done | bytes 196624 | tf_op jit(solution)/shard_map/psum | solution.py:12
  121.2 1.7 scatter_fusion
  127.8 24.7 %all-gather.2 = bf16[1024,384]{0,1:T(8,128)(2,1)S(1)} all-gather(bf16[128,384]{0,1:T(8,128)(2,1)S(1)} %select_select_fusion.4), channel_id=4, replica_groups=mesh['pa'=8,'pb'=64] {'pa'}, dimensions={0}, use_global_device_ids=true | all-gather | bytes 884736 | tf_op jit(solution)/shard_map/all_gather | solution.py:33
  155.1 53.4 %all-gather.3 = bf16[1,1536,128]{2,1,0:T(8,128)(2,1)} all-gather(bf16[1,24,128]{2,1,0:T(8,128)(2,1)S(1)} %copy-done.9), channel_id=5, replica_groups=mesh['pa'=8,'pb'=64] {'pb'}, dimensions={1}, use_global_device_ids=true | all-gather | bytes 399360 | tf_op jit(solution)/shard_map/all_gather | solution.py:47
  209.1 22.6 %all-reduce.21.cloned.1.call-done = (bf16[128,384]{0,1:T(8,128)(2,1)}, bf16[128,384]{0,1:T(8,128)(2,1)}) async-done(((bf16[128,384]{0,1:T(8,128)(2,1)}, bf16[128,384]{0,1:T(8,128)(2,1)}), (bf16[128,384]{0,1:T(8,128)(2,1)}, bf16[128,384]{0,1:T(8,128)(2,1)})) %all-reduce.21.cloned.1.call-update) | async-done | bytes 196624 | tf_op jit(solution)/shard_map/psum | solution.py:12
  232.7 1.9 scatter_fusion.1
  239.5 24.5 %all-gather.4 = bf16[1024,384]{0,1:T(8,128)(2,1)S(1)} all-gather(bf16[128,384]{0,1:T(8,128)(2,1)S(1)} %select_select_fusion.3), channel_id=6, replica_groups=mesh['pa'=8,'pb'=64] {'pa'}, dimensions={0}, use_global_device_ids=true | all-gather | bytes 884736 | tf_op jit(solution)/shard_map/all_gather | solution.py:33
  266.5 53.6 %all-gather.5 = bf16[1,1536,128]{2,1,0:T(8,128)(2,1)} all-gather(bf16[1,24,128]{2,1,0:T(8,128)(2,1)S(1)} %copy-done.8), channel_id=7, replica_groups=mesh['pa'=8,'pb'=64] {'pb'}, dimensions={1}, use_global_device_ids=true | all-gather | bytes 399360 | tf_op jit(solution)/shard_map/all_gather | solution.py:47
  320.8 22.6 %all-reduce.19.cloned.1.call-done = (bf16[128,384]{0,1:T(8,128)(2,1)}, bf16[128,384]{0,1:T(8,128)(2,1)}) async-done(((bf16[128,384]{0,1:T(8,128)(2,1)}, bf16[128,384]{0,1:T(8,128)(2,1)}), (bf16[128,384]{0,1:T(8,128)(2,1)}, bf16[128,384]{0,1:T(8,128)(2,1)})) %all-reduce.19.cloned.1.call-update) | async-done | bytes 196624 | tf_op jit(solution)/shard_map/psum | solution.py:12
  344.4 1.7 scatter_fusion.2
  351.0 24.5 %all-gather.6 = bf16[1024,384]{0,1:T(8,128)(2,1)S(1)} all-gather(bf16[128,384]{0,1:T(8,128)(2,1)S(1)} %select_select_fusion.2), channel_id=8, replica_groups=mesh['pa'=8,'pb'=64] {'pa'}, dimensions={0}, use_global_device_ids=true | all-gather | bytes 884736 | tf_op jit(solution)/shard_map/all_gather | solution.py:33
  378.0 53.6 %all-gather.7 = bf16[1,1536,128]{2,1,0:T(8,128)(2,1)} all-gather(bf16[1,24,128]{2,1,0:T(8,128)(2,1)S(1)} %copy-done.7), channel_id=9, replica_groups=mesh['pa'=8,'pb'=64] {'pb'}, dimensions={1}, use_global_device_ids=true | all-gather | bytes 399360 | tf_op jit(solution)/shard_map/all_gather | solution.py:47
  432.3 22.6 %all-reduce.17.cloned.1.call-done = (bf16[128,384]{0,1:T(8,128)(2,1)}, bf16[128,384]{0,1:T(8,128)(2,1)}) async-done(((bf16[128,384]{0,1:T(8,128)(2,1)}, bf16[128,384]{0,1:T(8,128)(2,1)}), (bf16[128,384]{0,1:T(8,128)(2,1)}, bf16[128,384]{0,1:T(8,128)(2,1)})) %all-reduce.17.cloned.1.call-update) | async-done | bytes 196624 | tf_op jit(solution)/shard_map/psum | solution.py:12
  455.9 2.0 scatter_fusion.3
  462.7 24.5 %all-gather.8 = bf16[1024,384]{0,1:T(8,128)(2,1)S(1)} all-gather(bf16[128,384]{0,1:T(8,128)(2,1)S(1)} %select_select_fusion.1), channel_id=10, replica_groups=mesh['pa'=8,'pb'=64] {'pa'}, dimensions={0}, use_global_device_ids=true | all-gather | bytes 884736 | tf_op jit(solution)/shard_map/all_gather | solution.py:33
  489.8 53.6 %all-gather.9 = bf16[1,1536,128]{2,1,0:T(8,128)(2,1)} all-gather(bf16[1,24,128]{2,1,0:T(8,128)(2,1)S(1)} %get-tuple-element.107), channel_id=11, replica_groups=mesh['pa'=8,'pb'=64] {'pb'}, dimensions={1}, use_global_device_ids=true | all-gather | bytes 399360 | tf_op jit(solution)/shard_map/all_gather | solution.py:47
  543.4 23.2 %all-reduce.15.cloned.1.call-done = (bf16[128,384]{0,1:T(8,128)(2,1)}, bf16[128,384]{0,1:T(8,128)(2,1)}) async-done(((bf16[128,384]{0,1:T(8,128)(2,1)}, bf16[128,384]{0,1:T(8,128)(2,1)}), (bf16[128,384]{0,1:T(8,128)(2,1)}, bf16[128,384]{0,1:T(8,128)(2,1)})) %all-reduce.15.cloned.1.call-update) | async-done | bytes 196624 | tf_op jit(solution)/shard_map/psum | solution.py:12
  567.6 1.7 scatter_fusion.4
  574.1 24.5 %all-gather.10 = bf16[1024,384]{0,1:T(8,128)(2,1)S(1)} all-gather(bf16[128,384]{0,1:T(8,128)(2,1)S(1)} %select_select_fusion), channel_id=12, replica_groups=mesh['pa'=8,'pb'=64] {'pa'}, dimensions={0}, use_global_device_ids=true | all-gather | bytes 884736 | tf_op jit(solution)/shard_map/all_gather | solution.py:33
  601.1 49.0 %all-gather.11 = bf16[1,1536,128]{2,1,0:T(8,128)(2,1)S(1)} all-gather(bf16[1,24,128]{2,1,0:T(8,128)(2,1)S(1)} %get-tuple-element.102), channel_id=13, replica_groups=mesh['pa'=8,'pb'=64] {'pb'}, dimensions={1}, use_global_device_ids=true | all-gather | bytes 399360 | tf_op jit(solution)/shard_map/all_gather | solution.py:47
  650.2 27.8 %all-reduce.13.cloned.1.call-done = (bf16[128,384]{0,1:T(8,128)(2,1)}, bf16[128,384]{0,1:T(8,128)(2,1)}) async-done(((bf16[128,384]{0,1:T(8,128)(2,1)}, bf16[128,384]{0,1:T(8,128)(2,1)}), (bf16[128,384]{0,1:T(8,128)(2,1)}, bf16[128,384]{0,1:T(8,128)(2,1)})) %all-reduce.13.cloned.1.call-update) | async-done | bytes 196624 | tf_op jit(solution)/shard_map/psum | solution.py:12
  679.0 1.7 scatter_fusion.5
  (165 shorter events, 58.7 us)
Async XLA Ops:
  6.5 113.7 %all-reduce.23.cloned.1.call-start = ((), (), s32[]{:S(2)}) async-start(), calls=%async_computation.5 | async-start | bytes 393216 | tf_op jit(solution)/shard_map/psum | solution.py:12
  37.9 6.2 copy-start.6
  41.1 190.6 %all-reduce.21.cloned.1.call-start = ((), (), s32[]{:S(2)}) async-start(), calls=%async_computation.4 | async-start | bytes 393216 | tf_op jit(solution)/shard_map/psum | solution.py:12
  126.0 1.8 copy-start.16
  126.0 1.8 copy-start.25
  152.5 2.6 copy-start.9
  152.7 55.8 %copy-start.30 = (s32[128]{0:T(128)S(1)}, s32[128]{0:T(128)}, u32[]{:S(2)}) copy-start(s32[128]{0:T(128)} %get-tuple-element.119) | copy-start | bytes 1540
  152.7 80.0 %copy-start.26 = (s32[128]{0:T(128)S(1)}, s32[128]{0:T(128)}, u32[]{:S(2)}) copy-start(s32[128]{0:T(128)} %get-tuple-element.125) | copy-start | bytes 1540
  155.0 188.3 %all-reduce.19.cloned.1.call-start = ((), (), s32[]{:S(2)}) async-start(), calls=%async_computation.3 | async-start | bytes 393216 | tf_op jit(solution)/shard_map/psum | solution.py:12
  237.6 1.8 copy-start.15
  237.7 1.8 copy-start.23
  263.9 2.6 copy-start.8
  264.1 56.0 %copy-start.29 = (s32[128]{0:T(128)S(1)}, s32[128]{0:T(128)}, u32[]{:S(2)}) copy-start(s32[128]{0:T(128)} %get-tuple-element.117) | copy-start | bytes 1540
  264.1 80.2 %copy-start.24 = (s32[128]{0:T(128)S(1)}, s32[128]{0:T(128)}, u32[]{:S(2)}) copy-start(s32[128]{0:T(128)} %get-tuple-element.126) | copy-start | bytes 1540
  266.5 188.4 %all-reduce.17.cloned.1.call-start = ((), (), s32[]{:S(2)}) async-start(), calls=%async_computation.2 | async-start | bytes 393216 | tf_op jit(solution)/shard_map/psum | solution.py:12
  349.1 1.8 copy-start.14
  375.4 2.6 copy-start.7
  375.6 56.0 %copy-start.28 = (s32[128]{0:T(128)S(1)}, s32[128]{0:T(128)}, u32[]{:S(2)}) copy-start(s32[128]{0:T(128)} %get-tuple-element.115) | copy-start | bytes 1540
  375.6 80.2 %copy-start.22 = (s32[128]{0:T(128)S(1)}, s32[128]{0:T(128)}, u32[]{:S(2)}) copy-start(s32[128]{0:T(128)} %get-tuple-element.127) | copy-start | bytes 1540
  378.0 188.6 %all-reduce.15.cloned.1.call-start = ((), (), s32[]{:S(2)}) async-start(), calls=%async_computation.1 | async-start | bytes 393216 | tf_op jit(solution)/shard_map/psum | solution.py:12
  487.4 56.0 %copy-start.27 = (s32[128]{0:T(128)S(1)}, s32[128]{0:T(128)}, u32[]{:S(2)}) copy-start(s32[128]{0:T(128)} %get-tuple-element.91) | copy-start | bytes 1540
  487.4 80.2 %copy-start.20 = (s32[128]{0:T(128)S(1)}, s32[128]{0:T(128)}, u32[]{:S(2)}) copy-start(s32[128]{0:T(128)} %get-tuple-element.128) | copy-start | bytes 1540
  489.7 188.3 %all-reduce.13.cloned.1.call-start = ((), (), s32[]{:S(2)}) async-start(), calls=%async_computation | async-start | bytes 393216 | tf_op jit(solution)/shard_map/psum | solution.py:12
  598.8 80.2 %copy-start.18 = (s32[128]{0:T(128)S(1)}, s32[128]{0:T(128)}, u32[]{:S(2)}) copy-start(s32[128]{0:T(128)} %get-tuple-element.124) | copy-start | bytes 1540
  (13 other events, 19.3 us)
Sparse Core Ops, SparseCore 0:
  41.2 78.9 all-reduce.22
  155.1 76.5 all-reduce.20
  266.6 76.7 all-reduce.18
  378.1 76.7 all-reduce.16
  489.8 76.7 all-reduce.14
  601.2 76.7 all-reduce.12
